TPU v7x, 256 devices: a whole 4x4x8 slice. The times are simulated.
256 devices in a mesh: section: 2 (over core), req: 16 (over x, y), head: 8 (over z).
Axes of the slice: x: 4, y: 4, z: 8, core: 2. Of those that a mesh axis runs over, the one named last changes fastest.
Arguments:
- tokens: bfloat16 [256, 8192], P(None, 'req'), may hold values from -14 to 14
- attention_gain: bfloat16 [2, 8192], P('section', 'req'), may hold values from 0.099609375 to 1.8984375
- query_key_value_weight: bfloat16 [2, 8192, 8, 1280], P('section', 'req', 'head'), may hold values from -0.0625 to 0.0625
- head_output_weight: bfloat16 [2, 8, 1024, 8192], P('section', 'head', None, 'req'), may hold values from -0.0625 to 0.0625
- feedforward_gain: bfloat16 [2, 8192], P('section', 'req'), may hold values from 0.099609375 to 1.8984375
- gate_up: bfloat16 [2, 8192, 2, 14336], P('section', 'req', None, 'head'), may hold values from -0.0625 to 0.0625
- down_weight: bfloat16 [2, 14336, 8192], P('section', 'head', 'req'), may hold values from -0.046875 to 0.046875
- packed_cache: bfloat16 [2, 32768, 8, 256], P('section', 'req', 'head'), may hold values from -70 to 70
- long_cache: bfloat16 [2, 2, 32768, 8, 256], P('section', None, 'req', 'head'), may hold values from -70 to 70
- lengths: int32 [16, 16], P('req'), may hold values from 1 to 256, 2048 in all within a row
- long_split: int32 [2, 16], P(None, 'req'), may hold values from 1 to 2048, 16384 in all within a row
Outputs:
- layer_outputs: bfloat16 [2, 256, 8192], P('section', None, 'req')
Inputs may be any that keep to these rules, and one draw needn't show every extreme that they name: Row g holds the lengths of the 16 requests of request group g in order; they sum to 2048, and the requests' keys fill that group's 2048 slots of packed_cache one request after another. `long_split`: entry (j, g) counts the live slots, the first ones, of group g's 2048 slots of long request j; each row sums to 16384.
All inputs are finite; a program needn't handle non-finite values.
Results may differ from a plain program's by a relative error of at most 0.04.
Values may be sent and summed in bfloat16 or wider, within the bound.
A program may use at most 64 MiB of HBM per device.

v0:
```python
import math
import jax
import jax.numpy as jnp
from jax import lax
from jax.sharding import PartitionSpec as P

MODEL_WIDTH = 8192
QUERY_HEADS = 64
KEY_VALUE_HEADS = 8
HEAD_SIZE = 128
LONG = 16384
EPSILON = 1e-05


def merged(part, axis, combine):
    gathered = jax.tree.map(lambda a: lax.all_gather(a, axis), part)

    def take(source):
        return jax.tree.map(lambda a: lax.dynamic_index_in_dim(a, source, 0, False), gathered)

    return lax.fori_loop(
        1, lax.axis_size(axis), lambda source, state: combine(state, take(source)), take(0)
    )


def shifted(value, axis, by):
    peers = lax.axis_size(axis)
    pairs = [(i, i + by) for i in range(peers) if 0 <= i + by < peers]
    return lax.ppermute(value, axis, pairs)


def rotate(values, position):
    half_dim = values.shape[-1] // 2
    freq_ids = jnp.arange(half_dim).astype(jnp.float32)
    inverse = 1.0 / 10000.0 ** (freq_ids * 2.0 / values.shape[-1])
    angles = position.astype(jnp.float32)[:, None] * inverse[None, :]
    cosine = jnp.cos(angles)[:, None, None, :]
    sine_part = jnp.sin(angles)[:, None, None, :]
    lower_half = values[..., :half_dim]
    upper_half = values[..., half_dim:]
    return jnp.concatenate(
        [
            lower_half * cosine - upper_half * sine_part,
            upper_half * cosine + lower_half * sine_part,
        ],
        -1,
    )


def add_pair(earlier, second_part):
    return earlier + second_part


def combine_partial(earlier, second_part):
    peak = jnp.maximum(earlier[0], second_part[0])
    left_factor = jnp.exp(earlier[0] - peak)
    right_factor = jnp.exp(second_part[0] - peak)
    softmax_total = earlier[1] * left_factor + second_part[1] * right_factor
    weighted_sum = earlier[2] * left_factor[..., None] + second_part[2] * right_factor[..., None]
    return (peak, softmax_total, weighted_sum)


def over_requests(values, combiner):
    return merged(values, "req", combiner)


def rows_apply(values, row_fn):
    return row_fn(lax.all_gather(values, "req", axis=0, tiled=True), jnp.int32(0))


def rows_project(term_fn, row_count):
    return lax.psum_scatter(
        term_fn(jnp.int32(0), row_count * lax.axis_size("req")),
        "req",
        scatter_dimension=0,
        tiled=True,
    )


def head_total(values):
    return lax.psum(values, "head")


def keep_rows(piece_rows, start_row):
    return piece_rows


def norm_rows(values, gain_row):
    floats = values.astype(jnp.float32)
    squares = over_requests(jnp.sum(floats * floats, axis=-1), add_pair)
    return (
        floats * lax.rsqrt(squares / MODEL_WIDTH + EPSILON)[:, None] * gain_row.astype(jnp.float32)
    ).astype(jnp.bfloat16)


def decoder_layer(
    inputs,
    micro_batch,
    attention_gain,
    query_key_value_weight,
    head_output_weight,
    feedforward_gain,
    gate_up,
    down_weight,
    packed_cache,
    long_cache,
    lengths,
    long_split,
):
    req_count = lax.axis_size("req")
    group_index = lax.axis_index("req")
    blocks = inputs.shape[0] // req_count
    columns = query_key_value_weight.shape[1]
    kv_local = query_key_value_weight.shape[2]
    requests_per_group = QUERY_HEADS // KEY_VALUE_HEADS
    score_scale = 1.0 / math.sqrt(HEAD_SIZE)
    normalized_input = norm_rows(inputs, attention_gain[0])
    in_weights = query_key_value_weight[0].reshape(
        columns, kv_local * (requests_per_group + 2) * HEAD_SIZE
    )

    def qkv_term(start_row, row_count):
        return jnp.dot(normalized_input, in_weights, preferred_element_type=jnp.float32)

    projected_rows = rows_project(qkv_term, blocks).reshape(
        blocks, kv_local, requests_per_group + 2, HEAD_SIZE
    )
    local_rows = jnp.arange(blocks)
    row_lengths = lengths[0]
    owner_long = (group_index == 0) | (group_index == req_count // 2)
    long_row = (local_rows == 0) & (micro_batch == 0) & owner_long
    position = row_lengths + jnp.where(long_row, LONG, 0).astype(jnp.int32)
    queries = rotate(projected_rows[:, :, :requests_per_group], position).astype(jnp.bfloat16)
    new_key = rotate(projected_rows[:, :, requests_per_group : requests_per_group + 1], position)[
        :, :, 0
    ].astype(jnp.bfloat16)
    new_value = projected_rows[:, :, requests_per_group + 1].astype(jnp.bfloat16)
    gathered = rows_apply(
        queries[0:1].reshape(1, kv_local * requests_per_group * HEAD_SIZE), keep_rows
    )
    long_queries = jnp.stack([gathered[0], gathered[req_count // 2]]).reshape(
        2, kv_local, requests_per_group, HEAD_SIZE
    )
    far_cache = long_cache[0]
    far_live = (jnp.arange(far_cache.shape[1])[None, :] < long_split[:, 0][:, None])[
        :, None, None, :
    ]
    far_scores = (
        jnp.einsum(
            "jkhd,jpkd->jkhp",
            long_queries,
            far_cache[..., :HEAD_SIZE],
            preferred_element_type=jnp.float32,
        )
        * score_scale
    )
    far_max = jnp.max(jnp.where(far_live, far_scores, -jnp.inf), axis=-1)
    far_weights = jnp.where(
        far_live, jnp.exp(jnp.where(far_live, far_scores - far_max[..., None], 0.0)), 0.0
    ).astype(jnp.bfloat16)
    far_totals = jnp.sum(far_weights.astype(jnp.float32), axis=-1)
    far_summed = jnp.einsum(
        "jkhp,jpkd->jkhd",
        far_weights,
        far_cache[..., HEAD_SIZE:],
        preferred_element_type=jnp.float32,
    )
    far_max, far_totals, far_summed = over_requests(
        (far_max, far_totals, far_summed), combine_partial
    )
    far_index = jnp.where(group_index == 0, 0, 1)
    chosen_max = lax.dynamic_index_in_dim(far_max, far_index, 0, keepdims=False)
    chosen_totals = lax.dynamic_index_in_dim(far_totals, far_index, 0, keepdims=False)
    chosen_summed = lax.dynamic_index_in_dim(far_summed, far_index, 0, keepdims=False)
    pack_part = packed_cache[0]
    seg_ends = jnp.cumsum(lengths[0])
    slot_ids = jnp.arange(pack_part.shape[0])
    slot_owner = jnp.sum((slot_ids[:, None] >= seg_ends[None, :]).astype(jnp.int32), axis=1)
    request_ids = micro_batch * blocks + local_rows
    in_segment = (slot_owner[None, :] == request_ids[:, None])[:, None, None, :]
    scores = (
        jnp.einsum(
            "rkhd,pkd->rkhp",
            queries,
            pack_part[..., :HEAD_SIZE],
            preferred_element_type=jnp.float32,
        )
        * score_scale
    )
    own_score = (
        jnp.einsum("rkhd,rkd->rkh", queries, new_key, preferred_element_type=jnp.float32)
        * score_scale
    )
    row_max = jnp.maximum(jnp.max(jnp.where(in_segment, scores, -jnp.inf), axis=-1), own_score)
    long_mask = long_row[:, None, None]
    row_max = jnp.where(long_mask, jnp.maximum(row_max, chosen_max[None]), row_max)
    weights = jnp.where(
        in_segment, jnp.exp(jnp.where(in_segment, scores - row_max[..., None], 0.0)), 0.0
    ).astype(jnp.bfloat16)
    own_weights = jnp.exp(own_score - row_max).astype(jnp.bfloat16)
    far_factor = jnp.where(
        long_mask, jnp.exp(jnp.where(long_mask, chosen_max[None] - row_max, 0.0)), 0.0
    )
    softmax_total = (
        jnp.sum(weights.astype(jnp.float32), axis=-1)
        + own_weights.astype(jnp.float32)
        + far_factor * chosen_totals[None]
    )
    weighted_sum = jnp.einsum(
        "rkhp,pkd->rkhd", weights, pack_part[..., HEAD_SIZE:], preferred_element_type=jnp.float32
    )
    weighted_sum = (
        weighted_sum
        + own_weights.astype(jnp.float32)[..., None] * new_value.astype(jnp.float32)[:, :, None, :]
    )
    weighted_sum = weighted_sum + far_factor[..., None] * chosen_summed[None]
    attended_heads = (
        (weighted_sum / softmax_total[..., None])
        .astype(jnp.bfloat16)
        .reshape(blocks, kv_local * requests_per_group * HEAD_SIZE)
    )
    out_weights = head_output_weight[0].reshape(kv_local * requests_per_group * HEAD_SIZE, columns)

    def project_heads(piece_rows, start_row):
        return jnp.dot(piece_rows, out_weights, preferred_element_type=jnp.float32)

    attended = head_total(rows_apply(attended_heads, project_heads))
    residual = (inputs.astype(jnp.float32) + attended).astype(jnp.bfloat16)
    normed_two = norm_rows(residual, feedforward_gain[0])
    ff_weights = gate_up[0].reshape(columns, -1)

    def ff_term(start_row, row_count):
        return jnp.dot(normed_two, ff_weights, preferred_element_type=jnp.float32)

    gate_and_up = rows_project(ff_term, blocks)
    hidden_width = gate_and_up.shape[1] // 2
    hidden = (jax.nn.silu(gate_and_up[:, :hidden_width]) * gate_and_up[:, hidden_width:]).astype(
        jnp.bfloat16
    )
    lower_weights = down_weight[0]

    def project_hidden(piece_rows, start_row):
        return jnp.dot(piece_rows, lower_weights, preferred_element_type=jnp.float32)

    lowered = head_total(rows_apply(hidden, project_hidden))
    return (residual.astype(jnp.float32) + lowered).astype(jnp.bfloat16)


def local(
    tokens,
    attention_gain,
    query_key_value_weight,
    head_output_weight,
    feedforward_gain,
    gate_up,
    down_weight,
    packed_cache,
    long_cache,
    lengths,
    long_split,
):
    req_count = lax.axis_size("req")
    section_index = lax.axis_index("section")
    batch_count = 1
    per_group = tokens.shape[0] // req_count
    blocks = per_group // batch_count
    columns = tokens.shape[1]
    token_grid = tokens.reshape(req_count, per_group, columns)
    result = jnp.zeros_like(token_grid)
    incoming = jnp.zeros((req_count * blocks, columns), jnp.bfloat16)
    for phase_step in range(batch_count + 1):
        micro_batch = phase_step - section_index
        is_active = (micro_batch >= 0) & (micro_batch < batch_count)
        micro_batch = jnp.clip(micro_batch, 0, batch_count - 1)
        new_batch = token_grid.reshape(req_count * blocks, columns)
        inputs = jnp.where(section_index == 0, new_batch, incoming)
        output = decoder_layer(
            inputs,
            micro_batch,
            attention_gain,
            query_key_value_weight,
            head_output_weight,
            feedforward_gain,
            gate_up,
            down_weight,
            packed_cache,
            long_cache,
            lengths,
            long_split,
        )
        placed = output.reshape(req_count, blocks, columns)
        result = jnp.where(is_active, placed, result)
        if phase_step < batch_count:
            incoming = shifted(output, "section", 1)
    return result.reshape(1, req_count * per_group, columns)


def solution(mesh):
    placed = (
        P(None, "req"),
        P("section", "req"),
        P("section", "req", "head", None),
        P("section", "head", None, "req"),
        P("section", "req"),
        P("section", "req", None, "head"),
        P("section", "head", "req"),
        P("section", "req", "head", None),
        P("section", None, "req", "head", None),
        P("req", None),
        P(None, "req"),
    )
    return jax.shard_map(
        local, mesh=mesh, in_specs=placed, out_specs=P("section", None, "req"), check_vma=False
    )
```

profile of v0, /device:TPU:2, one launch (start us, length us, event | category | flops | bytes accessed | tf_op | source)
XLA Modules:
  0.0 1032.9 jit_solution(9253363095233518662)
XLA Ops:
  7.8 23.3 %all-gather.10 = f32[16,1,256]{2,1,0:T(1,128)S(1)} all-gather(f32[1,1,256]{2,1,0:T(1,128)S(1)} %bitcast.379), channel_id=2, replica_groups=mesh['section'=2,'req'=16,'head'=8] {'req'}, dimensions={0}, use_global_device_ids=true | all-gather | bytes 17408 | tf_op jit(solution)/shard_map/all_gather | solution.py:16
  36.4 78.1 %reduce-scatter.5.cloned.1.call-done = f32[16,1280]{1,0:T(8,128)} async-done(((f32[256,1280]{1,0:T(8,128)}), f32[16,1280]{1,0:T(8,128)}) %reduce-scatter.5.cloned.1.call-update) | async-done | bytes 81936 | tf_op jit(solution)/shard_map/reduce_scatter | solution.py:72
  115.7 21.4 %all-gather.11 = bf16[16,1,1024]{2,1,0:T(2,128)(2,1)S(1)} all-gather(bf16[1,1,1024]{2,1,0:T(2,128)(2,1)S(1)} %reshape.774), channel_id=1, replica_groups=mesh['section'=2,'req'=16,'head'=8] {'req'}, dimensions={0}, use_global_device_ids=true | all-gather | bytes 34816 | tf_op jit(solution)/shard_map/all_gather | solution.py:68
  140.6 22.6 %all-gather.12 = f32[16,2,8]{2,1,0:T(2,128)S(1)} all-gather(f32[1,2,8]{2,1,0:T(2,128)S(1)} %bitcast.371), channel_id=3, replica_groups=mesh['section'=2,'req'=16,'head'=8] {'req'}, dimensions={0}, use_global_device_ids=true | all-gather | bytes 1088 | tf_op jit(solution)/shard_map/all_gather | solution.py:16
  163.2 21.1 %all-gather.13 = f32[16,2,8]{2,1,0:T(2,128)S(1)} all-gather(f32[1,2,8]{2,1,0:T(2,128)S(1)} %bitcast.375), channel_id=4, replica_groups=mesh['section'=2,'req'=16,'head'=8] {'req'}, dimensions={0}, use_global_device_ids=true | all-gather | bytes 1088 | tf_op jit(solution)/shard_map/all_gather | solution.py:16
  184.3 23.0 %all-gather.3 = f32[32,8,128]{2,1,0:T(8,128)S(1)} all-gather(f32[2,8,128]{2,1,0:T(8,128)S(1)} %fusion.33), channel_id=5, replica_groups=mesh['section'=2,'req'=16,'head'=8] {'req'}, dimensions={0}, use_global_device_ids=true | all-gather | bytes 139264 | tf_op jit(solution)/shard_map/all_gather | solution.py:16
  211.0 21.7 %all_gather.87 = bf16[256,1024]{1,0:T(8,128)(2,1)S(1)} all-gather(bf16[16,1024]{1,0:T(8,128)(2,1)S(1)} %bitcast.340), channel_id=1, replica_groups=mesh['section'=2,'req'=16,'head'=8] {'req'}, dimensions={0}, use_global_device_ids=true | all-gather | bytes 557056 | tf_op jit(solution)/shard_map/all_gather | solution.py:68
  238.6 69.5 %all-reduce.5.cloned.1.call-done = f32[256,512]{1,0:T(8,128)} async-done(((f32[256,512]{1,0:T(8,128)}), f32[256,512]{1,0:T(8,128)}) %all-reduce.5.cloned.1.call-update) | async-done | bytes 524304 | tf_op jit(solution)/shard_map/psum | solution.py:81
  309.3 23.0 %all-gather.14 = f32[16,1,256]{2,1,0:T(1,128)S(1)} all-gather(f32[1,1,256]{2,1,0:T(1,128)S(1)} %bitcast.378), channel_id=6, replica_groups=mesh['section'=2,'req'=16,'head'=8] {'req'}, dimensions={0}, use_global_device_ids=true | all-gather | bytes 17408 | tf_op jit(solution)/shard_map/all_gather | solution.py:16
  338.1 77.9 %reduce-scatter.7.cloned.1.call-done = f32[16,3584]{1,0:T(8,128)} async-done(((f32[256,3584]{1,0:T(8,128)}), f32[16,3584]{1,0:T(8,128)}) %reduce-scatter.7.cloned.1.call-update) | async-done | bytes 229392 | tf_op jit(solution)/shard_map/reduce_scatter | solution.py:72
  417.0 23.0 %all_gather.90 = bf16[256,1792]{1,0:T(8,128)(2,1)S(1)} all-gather(bf16[16,1792]{1,0:T(8,128)(2,1)S(1)} %fusion.70), channel_id=1, replica_groups=mesh['section'=2,'req'=16,'head'=8] {'req'}, dimensions={0}, use_global_device_ids=true | all-gather | bytes 974848 | tf_op jit(solution)/shard_map/all_gather | solution.py:68
  441.6 73.4 %all-reduce.7.cloned.1.call-done = f32[256,512]{1,0:T(8,128)} async-done(((f32[256,512]{1,0:T(8,128)}), f32[256,512]{1,0:T(8,128)}) %all-reduce.7.cloned.1.call-update) | async-done | bytes 524304 | tf_op jit(solution)/shard_map/psum | solution.py:81
  520.5 23.0 %all-gather.15 = f32[16,1,256]{2,1,0:T(1,128)S(1)} all-gather(f32[1,1,256]{2,1,0:T(1,128)S(1)} %bitcast.376), channel_id=7, replica_groups=mesh['section'=2,'req'=16,'head'=8] {'req'}, dimensions={0}, use_global_device_ids=true | all-gather | bytes 17408 | tf_op jit(solution)/shard_map/all_gather | solution.py:16
  546.8 74.6 %reduce-scatter.9.cloned.1.call-done = f32[16,1280]{1,0:T(8,128)} async-done(((f32[256,1280]{1,0:T(8,128)}), f32[16,1280]{1,0:T(8,128)}) %reduce-scatter.9.cloned.1.call-update) | async-done | bytes 81936 | tf_op jit(solution)/shard_map/reduce_scatter | solution.py:72
  622.6 21.5 %all-gather.16 = bf16[16,1,1024]{2,1,0:T(2,128)(2,1)S(1)} all-gather(bf16[1,1,1024]{2,1,0:T(2,128)(2,1)S(1)} %reshape.784), channel_id=1, replica_groups=mesh['section'=2,'req'=16,'head'=8] {'req'}, dimensions={0}, use_global_device_ids=true | all-gather | bytes 34816 | tf_op jit(solution)/shard_map/all_gather | solution.py:68
  649.5 22.6 %all-gather.17 = f32[16,2,8]{2,1,0:T(2,128)S(1)} all-gather(f32[1,2,8]{2,1,0:T(2,128)S(1)} %bitcast.370), channel_id=8, replica_groups=mesh['section'=2,'req'=16,'head'=8] {'req'}, dimensions={0}, use_global_device_ids=true | all-gather | bytes 1088 | tf_op jit(solution)/shard_map/all_gather | solution.py:16
  672.1 21.1 %all-gather.18 = f32[16,2,8]{2,1,0:T(2,128)S(1)} all-gather(f32[1,2,8]{2,1,0:T(2,128)S(1)} %bitcast.374), channel_id=9, replica_groups=mesh['section'=2,'req'=16,'head'=8] {'req'}, dimensions={0}, use_global_device_ids=true | all-gather | bytes 1088 | tf_op jit(solution)/shard_map/all_gather | solution.py:16
  693.2 22.9 %all-gather.8 = f32[32,8,128]{2,1,0:T(8,128)S(1)} all-gather(f32[2,8,128]{2,1,0:T(8,128)S(1)} %fusion.32), channel_id=10, replica_groups=mesh['section'=2,'req'=16,'head'=8] {'req'}, dimensions={0}, use_global_device_ids=true | all-gather | bytes 139264 | tf_op jit(solution)/shard_map/all_gather | solution.py:16
  719.9 22.1 %all_gather.100 = bf16[256,1024]{1,0:T(8,128)(2,1)S(1)} all-gather(bf16[16,1024]{1,0:T(8,128)(2,1)S(1)} %bitcast.341), channel_id=1, replica_groups=mesh['section'=2,'req'=16,'head'=8] {'req'}, dimensions={0}, use_global_device_ids=true | all-gather | bytes 557056 | tf_op jit(solution)/shard_map/all_gather | solution.py:68
  743.4 73.8 %all-reduce.9.cloned.1.call-done = f32[256,512]{1,0:T(8,128)} async-done(((f32[256,512]{1,0:T(8,128)}), f32[256,512]{1,0:T(8,128)}) %all-reduce.9.cloned.1.call-update) | async-done | bytes 524304 | tf_op jit(solution)/shard_map/psum | solution.py:81
  818.4 23.0 %all-gather.19 = f32[16,1,256]{2,1,0:T(1,128)S(1)} all-gather(f32[1,1,256]{2,1,0:T(1,128)S(1)} %bitcast.377), channel_id=11, replica_groups=mesh['section'=2,'req'=16,'head'=8] {'req'}, dimensions={0}, use_global_device_ids=true | all-gather | bytes 17408 | tf_op jit(solution)/shard_map/all_gather | solution.py:16
  847.2 78.0 %reduce-scatter.11.cloned.1.call-done = f32[16,3584]{1,0:T(8,128)} async-done(((f32[256,3584]{1,0:T(8,128)}), f32[16,3584]{1,0:T(8,128)}) %reduce-scatter.11.cloned.1.call-update) | async-done | bytes 229392 | tf_op jit(solution)/shard_map/reduce_scatter | solution.py:72
  926.2 23.0 %all_gather.103 = bf16[256,1792]{1,0:T(8,128)(2,1)S(1)} all-gather(bf16[16,1792]{1,0:T(8,128)(2,1)S(1)} %fusion.69), channel_id=1, replica_groups=mesh['section'=2,'req'=16,'head'=8] {'req'}, dimensions={0}, use_global_device_ids=true | all-gather | bytes 974848 | tf_op jit(solution)/shard_map/all_gather | solution.py:68
  950.7 73.4 %all-reduce.11.cloned.1.call-done = f32[256,512]{1,0:T(8,128)} async-done(((f32[256,512]{1,0:T(8,128)}), f32[256,512]{1,0:T(8,128)}) %all-reduce.11.cloned.1.call-update) | async-done | bytes 524304 | tf_op jit(solution)/shard_map/psum | solution.py:81
  (378 shorter events, 66.3 us)
Async XLA Ops:
  6.5 433.5 %copy-start = (bf16[1,1792,512]{2,1,0:T(8,128)(2,1)S(1)}, bf16[1,1792,512]{2,1,0:T(8,128)(2,1)}, u32[]{:S(2)}) copy-start(bf16[1,1792,512]{2,1,0:T(8,128)(2,1)} %param.29) | copy-start | bytes 5505028
  6.5 108.0 %reduce-scatter.5.cloned.1.call-start = ((), (), s32[]{:S(2)}) async-start(), calls=%async_computation.4 | async-start | bytes 1392640 | tf_op jit(solution)/shard_map/reduce_scatter | solution.py:72
  32.5 3.2 copy-start.9
  32.5 3.7 copy-start.10
  35.6 272.5 %all-reduce.5.cloned.1.call-start = ((), (), s32[]{:S(2)}) async-start(), calls=%async_computation.5 | async-start | bytes 1048576 | tf_op jit(solution)/shard_map/psum | solution.py:81
  35.9 173.5 %copy-start.7 = (bf16[1,2048,1,256]{3,1,2,0:T(8,128)(2,1)S(1)}, bf16[1,2048,1,256]{3,1,2,0:T(8,128)(2,1)}, u32[]{:S(2)}) copy-start(bf16[1,2048,1,256]{3,1,2,0:T(8,128)(2,1)} %param.30) | copy-start | bytes 3145732
  210.1 22.7 %copy-start.3 = (bf16[1,1,1024,512]{3,2,1,0:T(8,128)(2,1)S(1)}, bf16[1,1,1024,512]{3,2,1,0:T(8,128)(2,1)}, u32[]{:S(2)}) copy-start(bf16[1,1,1024,512]{3,2,1,0:T(8,128)(2,1)} %param.26) | copy-start | bytes 3145732
  234.0 182.0 %reduce-scatter.7.cloned.1.call-start = ((), (), s32[]{:S(2)}) async-start(), calls=%async_computation.6 | async-start | bytes 3899392 | tf_op jit(solution)/shard_map/reduce_scatter | solution.py:72
  234.1 4.5 copy-start.8
  234.1 74.0 %copy-start.2 = (bf16[256,512]{1,0:T(8,128)(2,1)S(1)}, bf16[256,512]{1,0:T(8,128)(2,1)}, u32[]{:S(2)}) copy-start(bf16[256,512]{1,0:T(8,128)(2,1)} %param.23) | copy-start | bytes 786436
  309.3 28.8 %copy-start.5 = (bf16[256,512]{1,0:T(8,128)(2,1)}, bf16[256,512]{1,0:T(8,128)(2,1)S(1)}, u32[]{:S(2)}) copy-start(bf16[256,512]{1,0:T(8,128)(2,1)S(1)} %get-tuple-element.859) | copy-start | bytes 786436
  338.1 176.9 %all-reduce.7.cloned.1.call-start = ((), (), s32[]{:S(2)}) async-start(), calls=%async_computation.7 | async-start | bytes 1048576 | tf_op jit(solution)/shard_map/psum | solution.py:81
  441.5 102.7 %copy-start.1 = (bf16[1,512,1,1280]{3,1,2,0:T(8,128)(2,1)S(1)}, bf16[1,512,1,1280]{3,1,2,0:T(8,128)(2,1)}, u32[]{:S(2)}) copy-start(bf16[1,512,1,1280]{3,1,2,0:T(8,128)(2,1)} %param.25) | copy-start | bytes 3932164
  441.5 179.9 %reduce-scatter.9.cloned.1.call-start = ((), (), s32[]{:S(2)}) async-start(), calls=%async_computation.8 | async-start | bytes 1392640 | tf_op jit(solution)/shard_map/reduce_scatter | solution.py:72
  516.9 2.8 collective-permute-start
  546.8 270.4 %all-reduce.9.cloned.1.call-start = ((), (), s32[]{:S(2)}) async-start(), calls=%async_computation.9 | async-start | bytes 1048576 | tf_op jit(solution)/shard_map/psum | solution.py:81
  717.9 24.1 %copy-start.4 = (bf16[1,1,1024,512]{3,2,1,0:T(8,128)(2,1)S(1)}, bf16[1,1,1024,512]{3,2,1,0:T(8,128)(2,1)}, u32[]{:S(2)}) copy-start(bf16[1,1,1024,512]{3,2,1,0:T(8,128)(2,1)} %param.26) | copy-start | bytes 3145732
  719.9 97.2 %copy-start.6 = (bf16[256,512]{1,0:T(8,128)(2,1)S(1)}, bf16[256,512]{1,0:T(8,128)(2,1)}, u32[]{:S(2)}) copy-start(bf16[256,512]{1,0:T(8,128)(2,1)} %get-tuple-element.857) | copy-start | bytes 786436
  743.3 181.8 %reduce-scatter.11.cloned.1.call-start = ((), (), s32[]{:S(2)}) async-start(), calls=%async_computation.10 | async-start | bytes 3899392 | tf_op jit(solution)/shard_map/reduce_scatter | solution.py:72
  847.2 176.9 %all-reduce.11.cloned.1.call-start = ((), (), s32[]{:S(2)}) async-start(), calls=%async_computation.11 | async-start | bytes 1048576 | tf_op jit(solution)/shard_map/psum | solution.py:81
Sparse Core Ops, SparseCore 0:
  35.7 78.7 reduce-scatter.4
  234.1 73.8 all-reduce.4
  338.2 77.7 reduce-scatter.6
  441.6 73.2 all-reduce.6
  546.9 74.4 reduce-scatter.8
  743.4 73.6 all-reduce.8
  847.3 77.8 reduce-scatter.10
  950.8 73.2 all-reduce.10
where the time goes:
time: 1030 us
  waiting for transfers between devices  600 us (58%)
  blocking collectives  358 us (35%)
  matrix products  31.8 us (3%)
  other arithmetic  17.6 us (2%)
  between operations  13.9 us (1%)
    reduce_scatter x4, waiting for transfers between devices, rows_project(): lax.psum_scatter(term_fn(jnp.int32(0), row_count * lax.axis_size('req')),...  309 us
    psum x4, waiting for transfers between devices, head_total(): return lax.psum(values, 'head')  290 us
    all_gather x10, blocking collectives, merged(): gathered = jax.tree.map(lambda a: lax.all_gather(a, axis), part)  226 us
    all_gather x6, blocking collectives, rows_apply(): lax.all_gather(values, 'req', axis=0, tiled=True)  133 us
  transfers between devices with their start and end apart: 9, of which 9 were waited for; matrix products, arithmetic and copies ran while one was open for 1% of the time, Pallas kernels for 0%

commit v1 on v0

--- a/solution.py
+++ b/solution.py
@@ -65,7 +65,13 @@
 
 
 def rows_apply(values, row_fn):
-    return row_fn(lax.all_gather(values, "req", axis=0, tiled=True), jnp.int32(0))
+    solve_ends = lambda block_here: jnp.concatenate(
+        jax.lax.all_to_all(
+            jnp.stack([block_here for _ in range(jax.lax.axis_size("req"))], 0), "req", 0, 0
+        ),
+        0,
+    )
+    return row_fn(solve_ends(values), jnp.int32(0))
 
 
 def rows_project(term_fn, row_count):

time: 1030 us -> 987 us (0.958)
  blocking collectives: 358 us -> 288 us
  starting transfers between devices: 2.28 us -> 13.7 us
    all_gather x6 -> x0, blocking collectives: 133 us -> none  [rows_apply(): lax.all_gather(values, 'req', axis=0, tiled=True)]
    all_to_all x0 -> x4, blocking collectives: none -> 61.2 us  [rows_apply(): jax.lax.all_to_all(jnp.stack([block_here for _ in range(jax.lax.axis_size...]
    all_to_all x0 -> x2, starting transfers between devices: none -> 11.4 us  [rows_apply(): jax.lax.all_to_all(jnp.stack([block_here for _ in range(jax.lax.axis_size...]
  transfers between devices with their start and end apart: 9 -> 11, of which waited for: 9 -> 11; matrix products, arithmetic and copies ran while one was open for 1% -> 1% of each run, Pallas kernels for 0% -> 0%
where the time goes in v1:
time: 987 us; the launch traced here: 986 us
  waiting for transfers between devices  606 us (61%)
  blocking collectives  288 us (29%)
  matrix products  34.1 us (3%)
  other arithmetic  19.3 us (2%)
  between operations  13.9 us (1%)
  starting transfers between devices  13.7 us (1%)
    reduce_scatter x4, waiting for transfers between devices, rows_project(): lax.psum_scatter(term_fn(jnp.int32(0), row_count * lax.axis_size('req')),...  308 us
    psum x4, waiting for transfers between devices, head_total(): return lax.psum(values, 'head')  288 us
    all_gather x10, blocking collectives, merged(): gathered = jax.tree.map(lambda a: lax.all_gather(a, axis), part)  226 us
    all_to_all x4, blocking collectives, rows_apply(): jax.lax.all_to_all(jnp.stack([block_here for _ in range(jax.lax.axis_size...  61.2 us
  transfers between devices with their start and end apart: 11, of which 11 were waited for; matrix products, arithmetic and copies ran while one was open for 1% of the time, Pallas kernels for 0%

profile of v1, /device:TPU:2, one launch (start us, length us, event | category | flops | bytes accessed | tf_op | source)
XLA Modules:
  0.0 986.1 jit_solution(3263592667374714678)
XLA Ops:
  7.8 23.3 %all-gather.10 = f32[16,1,256]{2,1,0:T(1,128)S(1)} all-gather(f32[1,1,256]{2,1,0:T(1,128)S(1)} %bitcast.379), channel_id=2, replica_groups=mesh['section'=2,'req'=16,'head'=8] {'req'}, dimensions={0}, use_global_device_ids=true | all-gather | bytes 17408 | tf_op jit(solution)/shard_map/all_gather | solution.py:16
  36.4 78.2 %reduce-scatter.5.cloned.1.call-done = f32[16,1280]{1,0:T(8,128)} async-done(((f32[256,1280]{1,0:T(8,128)}), f32[16,1280]{1,0:T(8,128)}) %reduce-scatter.5.cloned.1.call-update) | async-done | bytes 81936 | tf_op jit(solution)/shard_map/reduce_scatter | solution.py:78
  117.9 5.7 all-to-all-start
  133.3 21.7 %all-gather.11 = f32[16,2,8]{2,1,0:T(2,128)S(1)} all-gather(f32[1,2,8]{2,1,0:T(2,128)S(1)} %bitcast.367), channel_id=3, replica_groups=mesh['section'=2,'req'=16,'head'=8] {'req'}, dimensions={0}, use_global_device_ids=true | all-gather | bytes 1088 | tf_op jit(solution)/shard_map/all_gather | solution.py:16
  155.0 21.4 %all-gather.12 = f32[16,2,8]{2,1,0:T(2,128)S(1)} all-gather(f32[1,2,8]{2,1,0:T(2,128)S(1)} %bitcast.375), channel_id=4, replica_groups=mesh['section'=2,'req'=16,'head'=8] {'req'}, dimensions={0}, use_global_device_ids=true | all-gather | bytes 1088 | tf_op jit(solution)/shard_map/all_gather | solution.py:16
  176.4 23.8 %all-gather.3 = f32[32,8,128]{2,1,0:T(8,128)S(1)} all-gather(f32[2,8,128]{2,1,0:T(8,128)S(1)} %fusion.33), channel_id=5, replica_groups=mesh['section'=2,'req'=16,'head'=8] {'req'}, dimensions={0}, use_global_device_ids=true | all-gather | bytes 139264 | tf_op jit(solution)/shard_map/all_gather | solution.py:16
  204.2 13.1 %all_to_all.30 = bf16[16,16,1024]{2,1,0:T(8,128)(2,1)S(1)} all-to-all(bf16[16,16,1024]{2,1,0:T(8,128)(2,1)S(1)} %stack.28), channel_id=1, replica_groups=mesh['section'=2,'req'=16,'head'=8] {'req'}, dimensions={0} | all-to-all | bytes 1048576 | tf_op jit(solution)/shard_map/all_to_all | solution.py:69
  223.2 68.7 %all-reduce.5.cloned.1.call-done = f32[256,512]{1,0:T(8,128)} async-done(((f32[256,512]{1,0:T(8,128)}), f32[256,512]{1,0:T(8,128)}) %all-reduce.5.cloned.1.call-update) | async-done | bytes 524304 | tf_op jit(solution)/shard_map/psum | solution.py:87
  293.1 23.0 %all-gather.13 = f32[16,1,256]{2,1,0:T(1,128)S(1)} all-gather(f32[1,1,256]{2,1,0:T(1,128)S(1)} %bitcast.378), channel_id=6, replica_groups=mesh['section'=2,'req'=16,'head'=8] {'req'}, dimensions={0}, use_global_device_ids=true | all-gather | bytes 17408 | tf_op jit(solution)/shard_map/all_gather | solution.py:16
  321.9 77.9 %reduce-scatter.7.cloned.1.call-done = f32[16,3584]{1,0:T(8,128)} async-done(((f32[256,3584]{1,0:T(8,128)}), f32[16,3584]{1,0:T(8,128)}) %reduce-scatter.7.cloned.1.call-update) | async-done | bytes 229392 | tf_op jit(solution)/shard_map/reduce_scatter | solution.py:78
  400.9 17.5 %all_to_all.31 = bf16[16,16,1792]{2,1,0:T(8,128)(2,1)S(1)} all-to-all(bf16[16,16,1792]{2,1,0:T(8,128)(2,1)S(1)} %stack.29), channel_id=1, replica_groups=mesh['section'=2,'req'=16,'head'=8] {'req'}, dimensions={0} | all-to-all | bytes 1835008 | tf_op jit(solution)/shard_map/all_to_all | solution.py:69
  419.9 73.1 %all-reduce.7.cloned.1.call-done = f32[256,512]{1,0:T(8,128)} async-done(((f32[256,512]{1,0:T(8,128)}), f32[256,512]{1,0:T(8,128)}) %all-reduce.7.cloned.1.call-update) | async-done | bytes 524304 | tf_op jit(solution)/shard_map/psum | solution.py:87
  498.5 23.0 %all-gather.14 = f32[16,1,256]{2,1,0:T(1,128)S(1)} all-gather(f32[1,1,256]{2,1,0:T(1,128)S(1)} %bitcast.376), channel_id=7, replica_groups=mesh['section'=2,'req'=16,'head'=8] {'req'}, dimensions={0}, use_global_device_ids=true | all-gather | bytes 17408 | tf_op jit(solution)/shard_map/all_gather | solution.py:16
  524.8 74.7 %reduce-scatter.9.cloned.1.call-done = f32[16,1280]{1,0:T(8,128)} async-done(((f32[256,1280]{1,0:T(8,128)}), f32[16,1280]{1,0:T(8,128)}) %reduce-scatter.9.cloned.1.call-update) | async-done | bytes 81936 | tf_op jit(solution)/shard_map/reduce_scatter | solution.py:78
  602.2 5.7 all-to-all-start.3
  617.6 21.7 %all-gather.15 = f32[16,2,8]{2,1,0:T(2,128)S(1)} all-gather(f32[1,2,8]{2,1,0:T(2,128)S(1)} %bitcast.366), channel_id=8, replica_groups=mesh['section'=2,'req'=16,'head'=8] {'req'}, dimensions={0}, use_global_device_ids=true | all-gather | bytes 1088 | tf_op jit(solution)/shard_map/all_gather | solution.py:16
  639.3 21.4 %all-gather.16 = f32[16,2,8]{2,1,0:T(2,128)S(1)} all-gather(f32[1,2,8]{2,1,0:T(2,128)S(1)} %bitcast.374), channel_id=9, replica_groups=mesh['section'=2,'req'=16,'head'=8] {'req'}, dimensions={0}, use_global_device_ids=true | all-gather | bytes 1088 | tf_op jit(solution)/shard_map/all_gather | solution.py:16
  660.8 24.0 %all-gather.8 = f32[32,8,128]{2,1,0:T(8,128)S(1)} all-gather(f32[2,8,128]{2,1,0:T(8,128)S(1)} %fusion.32), channel_id=10, replica_groups=mesh['section'=2,'req'=16,'head'=8] {'req'}, dimensions={0}, use_global_device_ids=true | all-gather | bytes 139264 | tf_op jit(solution)/shard_map/all_gather | solution.py:16
  688.7 13.1 %all_to_all.32 = bf16[16,16,1024]{2,1,0:T(8,128)(2,1)S(1)} all-to-all(bf16[16,16,1024]{2,1,0:T(8,128)(2,1)S(1)} %stack.34), channel_id=1, replica_groups=mesh['section'=2,'req'=16,'head'=8] {'req'}, dimensions={0} | all-to-all | bytes 1048576 | tf_op jit(solution)/shard_map/all_to_all | solution.py:69
  703.2 73.2 %all-reduce.9.cloned.1.call-done = f32[256,512]{1,0:T(8,128)} async-done(((f32[256,512]{1,0:T(8,128)}), f32[256,512]{1,0:T(8,128)}) %all-reduce.9.cloned.1.call-update) | async-done | bytes 524304 | tf_op jit(solution)/shard_map/psum | solution.py:87
  777.5 23.0 %all-gather.17 = f32[16,1,256]{2,1,0:T(1,128)S(1)} all-gather(f32[1,1,256]{2,1,0:T(1,128)S(1)} %bitcast.377), channel_id=11, replica_groups=mesh['section'=2,'req'=16,'head'=8] {'req'}, dimensions={0}, use_global_device_ids=true | all-gather | bytes 17408 | tf_op jit(solution)/shard_map/all_gather | solution.py:16
  806.4 77.7 %reduce-scatter.11.cloned.1.call-done = f32[16,3584]{1,0:T(8,128)} async-done(((f32[256,3584]{1,0:T(8,128)}), f32[16,3584]{1,0:T(8,128)}) %reduce-scatter.11.cloned.1.call-update) | async-done | bytes 229392 | tf_op jit(solution)/shard_map/reduce_scatter | solution.py:78
  885.2 17.5 %all_to_all.33 = bf16[16,16,1792]{2,1,0:T(8,128)(2,1)S(1)} all-to-all(bf16[16,16,1792]{2,1,0:T(8,128)(2,1)S(1)} %stack.35), channel_id=1, replica_groups=mesh['section'=2,'req'=16,'head'=8] {'req'}, dimensions={0} | all-to-all | bytes 1835008 | tf_op jit(solution)/shard_map/all_to_all | solution.py:69
  904.2 73.2 %all-reduce.11.cloned.1.call-done = f32[256,512]{1,0:T(8,128)} async-done(((f32[256,512]{1,0:T(8,128)}), f32[256,512]{1,0:T(8,128)}) %all-reduce.11.cloned.1.call-update) | async-done | bytes 524304 | tf_op jit(solution)/shard_map/psum | solution.py:87
  (387 shorter events, 81.0 us)
Async XLA Ops:
  6.5 411.9 %copy-start = (bf16[1,1792,512]{2,1,0:T(8,128)(2,1)S(1)}, bf16[1,1792,512]{2,1,0:T(8,128)(2,1)}, u32[]{:S(2)}) copy-start(bf16[1,1792,512]{2,1,0:T(8,128)(2,1)} %param.29) | copy-start | bytes 5505028
  6.5 108.0 %reduce-scatter.5.cloned.1.call-start = ((), (), s32[]{:S(2)}) async-start(), calls=%async_computation.10 | async-start | bytes 1392640 | tf_op jit(solution)/shard_map/reduce_scatter | solution.py:78
  32.5 3.1 copy-start.8
  32.5 3.6 copy-start.9
  117.9 11.9 %all-to-all-start = ((bf16[16,2,512]{2,1,0:T(2,128)(2,1)}), bf16[16,2,512]{2,1,0:T(2,128)(2,1)S(1)}, u32[]{:S(2)}, u32[]{:S(2)}) async-start(bf16[16,2,512]{2,1,0:T(2,128)(2,1)} %reshape.847), calls=%async_computation.1 | async-start | bytes 65536 | tf_op jit(solution)/shard_map/all_to_all | solution.py:69
  123.6 168.3 %all-reduce.5.cloned.1.call-start = ((), (), s32[]{:S(2)}) async-start(), calls=%async_computation.11 | async-start | bytes 1048576 | tf_op jit(solution)/shard_map/psum | solution.py:87
  202.6 14.8 %copy-start.3 = (bf16[1,1,1024,512]{3,2,1,0:T(8,128)(2,1)S(1)}, bf16[1,1,1024,512]{3,2,1,0:T(8,128)(2,1)}, u32[]{:S(2)}) copy-start(bf16[1,1,1024,512]{3,2,1,0:T(8,128)(2,1)} %param.26) | copy-start | bytes 3145732
  218.6 181.2 %reduce-scatter.7.cloned.1.call-start = ((), (), s32[]{:S(2)}) async-start(), calls=%async_computation.12 | async-start | bytes 3899392 | tf_op jit(solution)/shard_map/reduce_scatter | solution.py:78
  218.7 4.5 copy-start.7
  218.7 73.2 %copy-start.2 = (bf16[256,512]{1,0:T(8,128)(2,1)S(1)}, bf16[256,512]{1,0:T(8,128)(2,1)}, u32[]{:S(2)}) copy-start(bf16[256,512]{1,0:T(8,128)(2,1)} %param.23) | copy-start | bytes 786436
  293.1 28.8 %copy-start.5 = (bf16[256,512]{1,0:T(8,128)(2,1)}, bf16[256,512]{1,0:T(8,128)(2,1)S(1)}, u32[]{:S(2)}) copy-start(bf16[256,512]{1,0:T(8,128)(2,1)S(1)} %get-tuple-element.863) | copy-start | bytes 786436
  321.9 171.1 %all-reduce.7.cloned.1.call-start = ((), (), s32[]{:S(2)}) async-start(), calls=%async_computation.13 | async-start | bytes 1048576 | tf_op jit(solution)/shard_map/psum | solution.py:87
  419.8 102.4 %copy-start.1 = (bf16[1,512,1,1280]{3,1,2,0:T(8,128)(2,1)S(1)}, bf16[1,512,1,1280]{3,1,2,0:T(8,128)(2,1)}, u32[]{:S(2)}) copy-start(bf16[1,512,1,1280]{3,1,2,0:T(8,128)(2,1)} %param.25) | copy-start | bytes 3932164
  419.8 179.7 %reduce-scatter.9.cloned.1.call-start = ((), (), s32[]{:S(2)}) async-start(), calls=%async_computation.14 | async-start | bytes 1392640 | tf_op jit(solution)/shard_map/reduce_scatter | solution.py:78
  494.9 2.8 collective-permute-start
  602.2 11.9 %all-to-all-start.3 = ((bf16[16,2,512]{2,1,0:T(2,128)(2,1)}), bf16[16,2,512]{2,1,0:T(2,128)(2,1)S(1)}, u32[]{:S(2)}, u32[]{:S(2)}) async-start(bf16[16,2,512]{2,1,0:T(2,128)(2,1)} %reshape.849), calls=%async_computation.6 | async-start | bytes 65536 | tf_op jit(solution)/shard_map/all_to_all | solution.py:69
  607.9 168.5 %all-reduce.9.cloned.1.call-start = ((), (), s32[]{:S(2)}) async-start(), calls=%async_computation.15 | async-start | bytes 1048576 | tf_op jit(solution)/shard_map/psum | solution.py:87
  687.1 14.8 %copy-start.4 = (bf16[1,1,1024,512]{3,2,1,0:T(8,128)(2,1)S(1)}, bf16[1,1,1024,512]{3,2,1,0:T(8,128)(2,1)}, u32[]{:S(2)}) copy-start(bf16[1,1,1024,512]{3,2,1,0:T(8,128)(2,1)} %param.26) | copy-start | bytes 3145732
  688.7 87.7 %copy-start.6 = (bf16[256,512]{1,0:T(8,128)(2,1)S(1)}, bf16[256,512]{1,0:T(8,128)(2,1)}, u32[]{:S(2)}) copy-start(bf16[256,512]{1,0:T(8,128)(2,1)} %get-tuple-element.861) | copy-start | bytes 786436
  703.1 181.0 %reduce-scatter.11.cloned.1.call-start = ((), (), s32[]{:S(2)}) async-start(), calls=%async_computation.16 | async-start | bytes 3899392 | tf_op jit(solution)/shard_map/reduce_scatter | solution.py:78
  806.3 171.0 %all-reduce.11.cloned.1.call-start = ((), (), s32[]{:S(2)}) async-start(), calls=%async_computation.17 | async-start | bytes 1048576 | tf_op jit(solution)/shard_map/psum | solution.py:87
Sparse Core Ops, SparseCore 0:
  35.7 78.7 reduce-scatter.4
  218.7 73.0 all-reduce.4
  322.0 77.7 reduce-scatter.6
  420.0 73.0 all-reduce.6
  524.9 74.5 reduce-scatter.8
  703.2 73.0 all-reduce.8
  806.5 77.6 reduce-scatter.10
  904.3 73.0 all-reduce.10
